TPU v7x, 512 devices: a whole 4x8x8 slice. The times are simulated.
512 devices in a mesh: node: 64 (over z_hi, y, core), local: 8 (over z_lo, x).
Axes of the slice: x: 4, y: 8, z: 8 (z_hi: 4, z_lo: 2; z = z_hi * 2 + z_lo), core: 2. Of those that a mesh axis runs over, the one named last changes fastest.
Arguments:
- block_input: bfloat16 [200704, 512], P(('node', 'local')), may hold values from 0 to 2
- conv_weight: bfloat16 [512, 2048], replicated, may hold values from -0.25 to 0.25
- bn_gain: float32 [2048], replicated, may hold values from 0.1 to 1.9
- out_cotangent: bfloat16 [200704, 2048], P(('node', 'local')), may hold values from -0.0546875 to 0.0546875
- master_weight: float32 [2048, 512], P('node'), may hold values from -0.25 to 0.25
- velocity: float32 [2048, 512], P('node'), may hold values from -6 to 6
Outputs:
- new_velocity: float32 [2048, 512], P('node')
- new_weight: float32 [2048, 512], P('node')
All inputs are finite; a program needn't handle non-finite values.
Results may differ from a plain program's by a relative error of at most 0.0095.
Values may be sent and summed in bfloat16 or wider, within the bound.
A program may use at most 64 MiB of HBM per device.

v0:
```python
import jax
import jax.numpy as jnp
from jax import lax
from jax.sharding import PartitionSpec as P

BUCKETS = 4


EPS = 1e-05
MOMENTUM = 0.9
RATE = 0.1
DECAY = 5e-05


def normalize_backward(block_input, conv_weight, bn_gain, out_cotangent):
    row_count = block_input.shape[0]
    convolved = jnp.dot(block_input, conv_weight, preferred_element_type=jnp.float32)
    center = jnp.mean(convolved, axis=0)
    spread = convolved - center
    inverse = lax.rsqrt(jnp.mean(spread * spread, axis=0) + EPS)
    normed = spread * inverse
    upstream = out_cotangent.astype(jnp.float32)
    shift_grad = jnp.sum(upstream, axis=0)
    gain_grad = jnp.sum(upstream * normed, axis=0)
    return (
        bn_gain * inverse / row_count * (row_count * upstream - shift_grad - normed * gain_grad)
    ).astype(jnp.bfloat16)


def reduce_shards(contribution):
    summed = lax.psum(contribution.astype(jnp.bfloat16), "local").astype(jnp.float32)
    return lax.psum_scatter(summed, "node", scatter_dimension=1, tiled=True)


def local(block_input, conv_weight, bn_gain, out_cotangent, master_weight, velocity):
    conv_grad = normalize_backward(block_input, conv_weight, bn_gain, out_cotangent)
    row_count = conv_grad.shape[0]
    width_out = conv_grad.shape[1]
    width_in = block_input.shape[1]
    node_count = lax.axis_size("node")
    node_rows = width_out // node_count
    bucket_rows = node_rows // BUCKETS
    ordered = conv_grad.reshape(row_count, node_count, BUCKETS, bucket_rows).transpose(0, 2, 1, 3)
    contract = (((0,), (0,)), ((), ()))
    pieces = []
    for bucket in range(BUCKETS):
        columns = ordered[:, bucket].reshape(row_count, node_count * bucket_rows)
        contribution = lax.dot_general(
            columns, block_input, contract, preferred_element_type=jnp.float32
        )
        pieces.append(reduce_shards(contribution.reshape(1, node_count, bucket_rows, width_in)))
    reduced = jnp.concatenate(pieces, axis=0)
    gradient = reduced.reshape(node_rows, width_in)
    new_velocity = MOMENTUM * velocity + gradient + DECAY * master_weight
    new_weight = master_weight - RATE * new_velocity
    return (new_velocity, new_weight)


def solution(mesh):
    in_specs = (
        P(("node", "local"), None),
        P(),
        P(),
        P(("node", "local"), None),
        P("node", None),
        P("node", None),
    )
    out_specs = (P("node", None), P("node", None))
    return jax.shard_map(local, mesh=mesh, in_specs=in_specs, out_specs=out_specs, check_vma=False)
```

profile of v0, /device:TPU:1, one launch (start us, length us, event | category | flops | bytes accessed | tf_op | source)
XLA Modules:
  0.0 739.9 jit_solution(14414003540777218087)
XLA Ops:
  7.2 0.0 all-reduce.3.cloned.1.call-start
  7.2 1.5 copy-done
  8.8 2.0 fusion.16
  10.8 0.4 multiply_reduce_fusion
  11.2 0.3 copy-done.7
  11.5 0.7 copy-done.1
  12.2 0.7 convert_reduce_fusion
  12.9 2.0 fusion.3
  15.0 3.8 copy.12
  18.7 2.3 fusion.8
  21.0 2.3 fusion.7
  23.3 2.3 fusion.6
  25.6 2.3 fusion.5
  27.9 0.0 all-reduce.3.cloned.1.call-update
  27.9 0.0 reduce-scatter.11.cloned.1.call-start
  28.0 95.2 %all-reduce.3.cloned.1.call-done = (bf16[1,64,8,512]{3,2,1,0:T(8,128)(2,1)}, bf16[1,64,8,512]{3,2,1,0:T(8,128)(2,1)}, bf16[1,64,8,512]{3,2,1,0:T(8,128)(2,1)}, bf16[1,64,8,512]{3,2,1,0:T(8,128)(2,1)}) async-done(((bf16[1,64,8,512]{3,2,1,0:T(8,128)(2,1)}, bf16[1,64,8,512]{3,2,1,0:T(8,128)(2,1)}, bf16[1,64,8,512]{3,2,1,0:T(8,128)(2,1)}, bf16[1,64,8,512]{3,2,1,0:T(8,128)(2,1)}), ...) | async-done | bytes 2097168 | tf_op jit(solution)/shard_map/psum | solution.py:31
  123.2 2.2 convert_element_type.55
  125.4 0.0 reduce-scatter.11.cloned.1.call-update
  125.4 0.0 reduce-scatter.9.cloned.1.call-start
  125.4 2.2 convert_element_type.52
  127.7 0.0 reduce-scatter.9.cloned.1.call-update
  127.7 0.0 reduce-scatter.7.cloned.1.call-start
  127.8 1.1 convert_element_type.49
  128.9 0.0 reduce-scatter.7.cloned.1.call-update
  128.9 0.0 reduce-scatter.5.cloned.1.call-start
  129.0 1.1 convert_element_type.46
  130.1 0.0 reduce-scatter.5.cloned.1.call-update
  130.1 147.2 %reduce-scatter.11.cloned.1.call-done = f32[1,1,8,512]{3,2,1,0:T(8,128)} async-done(((f32[1,64,8,512]{3,2,1,0:T(8,128)}), f32[1,1,8,512]{3,2,1,0:T(8,128)}) %reduce-scatter.11.cloned.1.call-update) | async-done | bytes 16400 | tf_op jit(solution)/shard_map/reduce_scatter | solution.py:32
  277.4 151.6 %reduce-scatter.9.cloned.1.call-done = f32[1,1,8,512]{3,2,1,0:T(8,128)} async-done(((f32[1,64,8,512]{3,2,1,0:T(8,128)}), f32[1,1,8,512]{3,2,1,0:T(8,128)}) %reduce-scatter.9.cloned.1.call-update) | async-done | bytes 16400 | tf_op jit(solution)/shard_map/reduce_scatter | solution.py:32
  429.0 151.5 %reduce-scatter.7.cloned.1.call-done = f32[1,1,8,512]{3,2,1,0:T(8,128)} async-done(((f32[1,64,8,512]{3,2,1,0:T(8,128)}), f32[1,1,8,512]{3,2,1,0:T(8,128)}) %reduce-scatter.7.cloned.1.call-update) | async-done | bytes 16400 | tf_op jit(solution)/shard_map/reduce_scatter | solution.py:32
  580.5 151.5 %reduce-scatter.5.cloned.1.call-done = f32[1,1,8,512]{3,2,1,0:T(8,128)} async-done(((f32[1,64,8,512]{3,2,1,0:T(8,128)}), f32[1,1,8,512]{3,2,1,0:T(8,128)}) %reduce-scatter.5.cloned.1.call-update) | async-done | bytes 16400 | tf_op jit(solution)/shard_map/reduce_scatter | solution.py:32
  731.9 1.4 multiply_subtract_fusion
  (15 shorter events, 0.0 us)
Async XLA Ops:
  7.2 1.6 copy-start
  7.2 116.0 %all-reduce.3.cloned.1.call-start = ((), (), s32[]{:S(2)}) async-start(), calls=%async_computation.8 | async-start | bytes 4194304 | tf_op jit(solution)/shard_map/psum | solution.py:31
  10.8 0.7 copy-start.7
  10.8 1.4 copy-start.1
  15.0 3.8 copy-start.2
  27.9 249.5 %reduce-scatter.11.cloned.1.call-start = ((), (), s32[]{:S(2)}) async-start(), calls=%async_computation.7 | async-start | bytes 1064960 | tf_op jit(solution)/shard_map/reduce_scatter | solution.py:32
  123.2 4.6 copy-start.4
  125.4 3.6 copy-start.3
  125.4 303.6 %reduce-scatter.9.cloned.1.call-start = ((), (), s32[]{:S(2)}) async-start(), calls=%async_computation.6 | async-start | bytes 1064960 | tf_op jit(solution)/shard_map/reduce_scatter | solution.py:32
  127.7 604.2 %copy-start.5 = (f32[32,512]{1,0:T(8,128)S(1)}, f32[32,512]{1,0:T(8,128)}, u32[]{:S(2)}) copy-start(f32[32,512]{1,0:T(8,128)} %param.10) | copy-start | bytes 196612
  127.7 604.2 %copy-start.6 = (f32[32,512]{1,0:T(8,128)S(1)}, f32[32,512]{1,0:T(8,128)}, u32[]{:S(2)}) copy-start(f32[32,512]{1,0:T(8,128)} %param.11) | copy-start | bytes 196612
  127.7 452.7 %reduce-scatter.7.cloned.1.call-start = ((), (), s32[]{:S(2)}) async-start(), calls=%async_computation.5 | async-start | bytes 1064960 | tf_op jit(solution)/shard_map/reduce_scatter | solution.py:32
  128.9 603.0 %reduce-scatter.5.cloned.1.call-start = ((), (), s32[]{:S(2)}) async-start(), calls=%async_computation.4 | async-start | bytes 1064960 | tf_op jit(solution)/shard_map/reduce_scatter | solution.py:32
Sparse Core Ops, SparseCore 0:
  28.0 95.0 all-reduce.2
  127.7 149.6 reduce-scatter.10
  281.9 147.0 reduce-scatter.8
  433.4 147.0 reduce-scatter.6
  584.9 147.0 reduce-scatter.4
where the time goes:
time: 744 us; the launch traced here: 740 us
  waiting for transfers between devices  697 us (94%)
  between operations  13.8 us (2%)
  other arithmetic  11.3 us (2%)
  matrix products  11.2 us (2%)
    reduce_scatter x4, waiting for transfers between devices, reduce_shards(): return lax.psum_scatter(summed, 'node', scatter_dimension=1, tiled=True)  602 us
    psum x1, waiting for transfers between devices, reduce_shards(): lax.psum(contribution.astype(jnp.bfloat16), 'local').astype(jnp.float32)  95.2 us
  transfers between devices with their start and end apart: 5, of which 5 were waited for; matrix products, arithmetic and copies ran while one was open for 1% of the time, Pallas kernels for 0%

commit v1 on v0

v1 whole, which is shorter than its diff:
```python
import jax
import jax.numpy as jnp
from jax import lax
from jax.experimental import pallas as pl
from jax.experimental.pallas import tpu as pltpu
from jax.sharding import PartitionSpec as P

EPS = 1e-05
MOMENTUM = 0.9
RATE = 0.1
DECAY = 5e-05
MESH = pl.DeviceIdType.MESH
FAR_FIRST = (4, 3, 5, 2, 6, 1, 7)
F32 = jnp.float32
BF16 = jnp.bfloat16


def normalize_backward(block_input, conv_weight, bn_gain, out_cotangent):
    row_count = block_input.shape[0]
    convolved = jnp.dot(block_input, conv_weight, preferred_element_type=F32)
    center = jnp.mean(convolved, axis=0)
    spread = convolved - center
    inverse = lax.rsqrt(jnp.mean(spread * spread, axis=0) + EPS)
    normed = spread * inverse
    upstream = out_cotangent.astype(F32)
    shift_grad = jnp.sum(upstream, axis=0)
    gain_grad = jnp.sum(upstream * normed, axis=0)
    return (
        bn_gain * inverse / row_count * (row_count * upstream - shift_grad - normed * gain_grad)
    ).astype(BF16)


def reduce_kernel(
    term, out, pair_a, pair_b, mine_a, mine_b, ring_a, ring_b, part_a, part_b, last_a, last_b, piece, pieces,
    pair_send, pair_recv, ring_send, ring_recv, last_send, last_recv, piece_send, piece_recv,
):
    node = lax.axis_index("node")
    place = lax.axis_index("local")
    core = lax.rem(node, 2)
    y = lax.rem(node // 2, 8)
    z = (node // 16) * 2 + place // 4
    x = lax.rem(place, 4)

    def device(to_z, to_y, to_core):
        return ((to_z // 2) * 16 + to_y * 2 + to_core, lax.rem(to_z, 2) * 4 + x)

    def y_at(d):
        return device(z, lax.rem(y + d, 8), core)

    def z_at(d):
        return device(lax.rem(z + d, 8), y, core)

    def place_at(k):
        return (node, lax.rem(place + k, 8))

    partner = device(z, y, 1 - core)
    barrier = pltpu.get_barrier_semaphore()
    peers = [partner] + [y_at(d) for d in range(1, 8)] + [z_at(d) for d in range(1, 8)]
    peers += [place_at(k) for k in range(1, 8)]
    for peer in peers:
        pl.semaphore_signal(barrier, inc=1, device_id=peer, device_id_type=MESH)
    pl.semaphore_wait(barrier, len(peers))

    def send(source, target, sends, recvs, slot, peer):
        copy = pltpu.make_async_remote_copy(
            src_ref=source, dst_ref=target, send_sem=sends.at[slot], recv_sem=recvs.at[slot],
            device_id=peer, device_id_type=MESH,
        )
        copy.start()
        return copy

    left, right = pl.ds(0, 256), pl.ds(256, 256)
    started = []
    pairs = {}
    for d in FAR_FIRST + (0,):
        to_y = lax.rem(y + d, 8)
        to_z = lax.rem(z + d, 8)
        pairs["a", d] = send(
            term.at[:, to_y, 1 - core, :, :, left], pair_a.at[d], pair_send.at[0], pair_recv.at[0], d, partner
        )
        pairs["b", d] = send(
            term.at[to_z // 2, :, 1 - core, lax.rem(to_z, 2), :, right], pair_b.at[d],
            pair_send.at[1], pair_recv.at[1], d, partner,
        )
    rings = {}
    for d in FAR_FIRST + (0,):
        to_y = lax.rem(y + d, 8)
        to_z = lax.rem(z + d, 8)
        pairs["a", d].wait_recv()

        @pl.loop(0, 4)
        def _(i):
            own = term[i, to_y, core, :, :, 0:256].astype(F32)
            mine_a[d, i] = (own + pair_a[d, i].astype(F32)).astype(BF16)

        if d:
            rings["a", d] = send(mine_a.at[d], ring_a.at[d - 1], ring_send.at[0], ring_recv.at[0], d - 1, y_at(d))
        pairs["b", d].wait_recv()

        @pl.loop(0, 8)
        def _(i):
            own = term[to_z // 2, i, core, lax.rem(to_z, 2), :, 256:512].astype(F32)
            mine_b[d, i] = (own + pair_b[d, i].astype(F32)).astype(BF16)

        if d:
            rings["b", d] = send(mine_b.at[d], ring_b.at[d - 1], ring_send.at[1], ring_recv.at[1], d - 1, z_at(d))

    for d in range(1, 8):
        rings["a", d].wait_recv()

    @pl.loop(0, 8)
    def _(i):
        total = mine_a[0, i // 2, lax.rem(i, 2)].astype(F32)
        for d in range(7):
            total += ring_a[d, i // 2, lax.rem(i, 2)].astype(F32)
        part_a[i] = total.astype(BF16)

    lasts = {}
    for d in FAR_FIRST:
        lasts["a", d] = send(
            part_a.at[lax.rem(z + d, 8)], last_a.at[d - 1], last_send.at[0], last_recv.at[0], d - 1, z_at(d)
        )
    for d in range(1, 8):
        rings["b", d].wait_recv()

    @pl.loop(0, 8)
    def _(i):
        total = mine_b[0, i].astype(F32)
        for d in range(7):
            total += ring_b[d, i].astype(F32)
        part_b[i] = total.astype(BF16)

    for d in FAR_FIRST:
        lasts["b", d] = send(
            part_b.at[lax.rem(y + d, 8)], last_b.at[d - 1], last_send.at[1], last_recv.at[1], d - 1, y_at(d)
        )
    for d in range(1, 8):
        lasts["a", d].wait_recv()
    total = part_a[z].astype(F32)
    for d in range(7):
        total += last_a[d].astype(F32)
    piece[:, 0:256] = total.astype(BF16)
    for d in range(1, 8):
        lasts["b", d].wait_recv()
    total = part_b[y].astype(F32)
    for d in range(7):
        total += last_b[d].astype(F32)
    piece[:, 256:512] = total.astype(BF16)
    ends = [send(piece, pieces.at[place], piece_send, piece_recv, k - 1, place_at(k)) for k in range(1, 8)]
    pieces[place] = piece[...]
    for copy in ends:
        copy.wait_recv()
    for half in range(2):
        total = pieces[half * 4].astype(F32)
        for i in range(1, 4):
            total += pieces[half * 4 + i].astype(F32)
        out[half] = total
    for copy in [*pairs.values(), *rings.values(), *lasts.values(), *ends]:
        copy.wait_send()


def reduce_terms(term):
    dma = pltpu.SemaphoreType.DMA
    return pl.pallas_call(
        reduce_kernel,
        out_shape=jax.ShapeDtypeStruct((2, 16, 512), F32),
        in_specs=[pl.BlockSpec(memory_space=pltpu.VMEM)],
        out_specs=pl.BlockSpec(memory_space=pltpu.VMEM),
        scratch_shapes=[
            pltpu.VMEM((8, 4, 2, 16, 256), BF16),
            pltpu.VMEM((8, 8, 16, 256), BF16),
            pltpu.VMEM((8, 4, 2, 16, 256), BF16),
            pltpu.VMEM((8, 8, 16, 256), BF16),
            pltpu.VMEM((7, 4, 2, 16, 256), BF16),
            pltpu.VMEM((7, 8, 16, 256), BF16),
            pltpu.VMEM((8, 16, 256), BF16),
            pltpu.VMEM((8, 16, 256), BF16),
            pltpu.VMEM((7, 16, 256), BF16),
            pltpu.VMEM((7, 16, 256), BF16),
            pltpu.VMEM((16, 512), BF16),
            pltpu.VMEM((8, 16, 512), BF16),
            dma((2, 8)), dma((2, 8)), dma((2, 7)), dma((2, 7)), dma((2, 7)), dma((2, 7)), dma((7,)), dma((7,)),
        ],
        compiler_params=pltpu.CompilerParams(collective_id=0, has_side_effects=True),
    )(term)


def local(block_input, conv_weight, bn_gain, out_cotangent, master_weight, velocity):
    conv_grad = normalize_backward(block_input, conv_weight, bn_gain, out_cotangent)
    term = lax.dot_general(conv_grad, block_input, (((0,), (0,)), ((), ())), preferred_element_type=F32)
    term = term.astype(BF16).reshape(4, 8, 2, 2, 16, 512)
    gradient = reduce_terms(term).reshape(32, 512)
    new_velocity = MOMENTUM * velocity + gradient + DECAY * master_weight
    new_weight = master_weight - RATE * new_velocity
    return (new_velocity, new_weight)


def solution(mesh):
    in_specs = (
        P(("node", "local"), None),
        P(),
        P(),
        P(("node", "local"), None),
        P("node", None),
        P("node", None),
    )
    out_specs = (P("node", None), P("node", None))
    return jax.shard_map(local, mesh=mesh, in_specs=in_specs, out_specs=out_specs, check_vma=False)
```

time: 744 us -> 51.5 us (0.07)
  waiting for transfers between devices: 697 us -> 0 us
  Pallas kernels: 0 us -> 40.4 us
  between operations: 13.8 us -> 0.72 us
  other arithmetic: 11.3 us -> 2.6 us
    reduce_scatter x4 -> x0, waiting for transfers between devices: 602 us -> none  [reduce_shards(): return lax.psum_scatter(summed, 'node', scatter_dimension=1, tiled=True)]
    psum x1 -> x0, waiting for transfers between devices: 95.2 us -> none  [reduce_shards(): lax.psum(contribution.astype(jnp.bfloat16), 'local').astype(jnp.float32)]
    pallas_call x0 -> x1, Pallas kernels: none -> 40.4 us  [reduce_terms(): pl.pallas_call(reduce_kernel, out_shape=jax.ShapeDtypeStruct((2, 16, 512)...]
    convert_element_type x5 -> x0, other arithmetic: 8.74 us -> none  [the longest x4 6.69 us: reduce_shards(): lax.psum(contribution.astype(jnp.bfloat16), 'local').astype(jnp.float32)]
  transfers between devices with their start and end apart: 5 -> 0, of which waited for: 5 -> 0; matrix products, arithmetic and copies ran while one was open for 1% -> 0% of each run, Pallas kernels for 0% -> 0%
where the time goes in v1:
time: 51.5 us; the launch traced here: 51.1 us
  Pallas kernels  40.4 us (78%)
  matrix products  4.77 us (9%)
  local copies, waits for them, and re-layouts  2.62 us (5%)
  other arithmetic  2.6 us (5%)
  between operations  0.72 us (1%)
    pallas_call x1, Pallas kernels, reduce_terms(): pl.pallas_call(reduce_kernel, out_shape=jax.ShapeDtypeStruct((2, 16, 512)...  40.4 us
    dot_general x1, matrix products, local(): lax.dot_general(conv_grad, block_input, (((0,), (0,)), ((), ())), preferr...  2.76 us
    unnamed x12, local copies, waits for them, and re-layouts  2.62 us
    dot_general x1, matrix products, normalize_backward(): convolved = jnp.dot(block_input, conv_weight, preferred_element_type=F32)  2.01 us
    sub x1, other arithmetic, local(): new_weight = master_weight - RATE * new_velocity  1.51 us

profile of v1, /device:TPU:1, one launch (start us, length us, event | category | flops | bytes accessed | tf_op | source)
XLA Modules:
  0.0 51.1 jit_solution(15101061394528092540)
XLA Ops:
  0.6 0.0 copy-start
  0.6 1.6 %copy-done = bf16[512,2048]{1,0:T(8,128)(2,1)S(1)} copy-done((bf16[512,2048]{1,0:T(8,128)(2,1)S(1)}, bf16[512,2048]{1,0:T(8,128)(2,1)}, u32[]{:S(2)}) %copy-start) | copy-done | bytes 2097176
  2.2 2.0 %fusion.15 = (f32[2048]{0:T(1024)S(1)}, f32[392,2048]{1,0:T(8,128)S(1)}) fusion(bf16[392,512]{1,0:T(8,128)(2,1)} %param.6, bf16[512,2048]{1,0:T(8,128)(2,1)S(1)} %copy-done), kind=kOutput, calls=%fused_computation.23 | convolution fusion | flops 822884352 | bytes 5718016 | tf_op jit(solution)/shard_map/dot_general | solution.py:20
  4.2 0.0 copy-start.5
  4.3 0.0 copy-start.1
  4.3 0.4 multiply_reduce_fusion
  4.7 0.3 copy-done.5
  4.9 0.0 copy-start.2
  5.0 0.7 %copy-done.1 = bf16[392,2048]{1,0:T(8,128)(2,1)S(1)} copy-done((bf16[392,2048]{1,0:T(8,128)(2,1)S(1)}, bf16[392,2048]{1,0:T(8,128)(2,1)}, u32[]{:S(2)}) %copy-start.1) | copy-done | bytes 1605656
  5.7 0.7 %convert_reduce_fusion = (f32[2048]{0:T(1024)S(1)}, f32[2048]{0:T(1024)S(1)}) fusion(bf16[392,2048]{1,0:T(8,128)(2,1)S(1)} %copy-done.1, f32[2048]{0:T(1024)S(1)} %get-tuple-element.7, f32[392,2048]{1,0:T(8,128)S(1)} %get-tuple-element.9, f32[2048]{0:T(1024)S(1)} %broadcast_multiply_fusion), kind=kLoop, calls=%fused_computation.1 | loop fusion | flops 4812800 | bytes 4849664 | tf_op jit(solution)/shard_map/reduce_sum | solution.py:26
  6.4 0.0 copy-done.2
  6.4 0.0 copy-start.3
  6.4 0.0 copy-start.4
  6.4 2.8 %convolution_convert_fusion = bf16[2048,512]{1,0:T(8,128)(2,1)} fusion(bf16[392,512]{1,0:T(8,128)(2,1)S(1)} %copy-done.2, bf16[392,2048]{1,0:T(8,128)(2,1)S(1)} %copy-done.1, f32[392,2048]{1,0:T(8,128)S(1)} %get-tuple-element.9, f32[2048]{0:T(1024)S(1)} %get-tuple-element.3, f32[2048]{0:T(1024)S(1)} %get-tuple-element.7, f32[2048]{0:T(1024)S(1)} %get-tuple-element.2, ...), kind=kOutput, calls=%fused_computation.9 | convolution fusion | flops 830357504 | bytes 7356416 | tf_op jit(solution)/shard_map/dot_general | solution.py:190
  9.2 40.4 %shard_map.77 = f32[2,16,512]{2,1,0:T(8,128)} custom-call(bf16[4,8,2,2,16,512]{5,4,3,2,1,0:T(8,128)(2,1)} %bitcast.9), custom_call_target="tpu_custom_call" | custom-call | tf_op jit(solution)/shard_map/pallas_call | solution.py:164
  49.6 0.0 copy-done.3
  49.6 0.0 copy-done.4
  49.6 1.5 %multiply_subtract_fusion = (f32[32,512]{1,0:T(8,128)}, f32[32,512]{1,0:T(8,128)}) fusion(f32[32,512]{1,0:T(8,128)S(1)} %copy-done.3, f32[2,16,512]{2,1,0:T(8,128)} %shard_map.77, f32[32,512]{1,0:T(8,128)S(1)} %copy-done.4), kind=kLoop, calls=%fused_computation.18 | loop fusion | flops 98304 | bytes 327680 | tf_op jit(solution)/shard_map/sub | solution.py:194
  (2 shorter events, 0.0 us)
Async XLA Ops:
  0.6 1.6 %copy-start = (bf16[512,2048]{1,0:T(8,128)(2,1)S(1)}, bf16[512,2048]{1,0:T(8,128)(2,1)}, u32[]{:S(2)}) copy-start(bf16[512,2048]{1,0:T(8,128)(2,1)} %param.7) | copy-start | bytes 6291460
  4.2 0.7 %copy-start.5 = (f32[2048]{0:T(1024)S(1)}, f32[2048]{0:T(1024)}, u32[]{:S(2)}) copy-start(f32[2048]{0:T(1024)} %param.8) | copy-start | bytes 24580
  4.3 1.4 %copy-start.1 = (bf16[392,2048]{1,0:T(8,128)(2,1)S(1)}, bf16[392,2048]{1,0:T(8,128)(2,1)}, u32[]{:S(2)}) copy-start(bf16[392,2048]{1,0:T(8,128)(2,1)} %param.9) | copy-start | bytes 4816900
  4.9 1.4 %copy-start.2 = (bf16[392,512]{1,0:T(8,128)(2,1)S(1)}, bf16[392,512]{1,0:T(8,128)(2,1)}, u32[]{:S(2)}) copy-start(bf16[392,512]{1,0:T(8,128)(2,1)} %param.6) | copy-start | bytes 1204228
  6.4 43.2 %copy-start.3 = (f32[32,512]{1,0:T(8,128)S(1)}, f32[32,512]{1,0:T(8,128)}, u32[]{:S(2)}) copy-start(f32[32,512]{1,0:T(8,128)} %param.10) | copy-start | bytes 196612
  6.4 43.2 %copy-start.4 = (f32[32,512]{1,0:T(8,128)S(1)}, f32[32,512]{1,0:T(8,128)}, u32[]{:S(2)}) copy-start(f32[32,512]{1,0:T(8,128)} %param.11) | copy-start | bytes 196612

commit v2 on v0

v2 whole, which is shorter than its diff:
```python
import jax
import jax.numpy as jnp
from jax import lax
from jax.experimental import pallas as pl
from jax.experimental.pallas import tpu as pltpu
from jax.sharding import PartitionSpec as P

EPS = 1e-05
MOMENTUM = 0.9
RATE = 0.1
DECAY = 5e-05
MESH = pl.DeviceIdType.MESH
FAR_FIRST = (4, 3, 5, 2, 6, 1, 7)
BLOCK_STEPS = (2, 1, 3, 0)
F32 = jnp.float32
BF16 = jnp.bfloat16
ROWS = 392
CIN = 512
WIDTH = 512


def conv_grad_of(x, weight, gain, cotangent):
    conv = jnp.dot(x, weight, preferred_element_type=F32)
    center = jnp.sum(conv, axis=0, keepdims=True) * (1.0 / ROWS)
    spread = conv - center
    inverse = lax.rsqrt(jnp.sum(spread * spread, axis=0, keepdims=True) * (1.0 / ROWS) + EPS)
    upstream = cotangent.astype(F32)
    shift_grad = jnp.sum(upstream, axis=0, keepdims=True)
    gain_grad = jnp.sum(upstream * spread, axis=0, keepdims=True) * inverse
    scale = gain * inverse / ROWS
    return (scale * (ROWS * upstream - shift_grad - spread * (inverse * gain_grad))).astype(BF16)


def step_kernel(
    x_hbm, weight_hbm, gain_hbm, cotangent_hbm, out, x, weight, gain, cotangent,
    term, pair, mine_a, mine_b, ring_a, ring_b, part_a, part_b, last_a, last_b, piece, pieces,
    x_sem, weight_sem, gain_sem, cotangent_sem, pair_send, pair_recv, ring_a_send, ring_a_recv, ring_b_send, ring_b_recv,
    last_send, last_recv, piece_send, piece_recv,
):
    node = lax.axis_index("node")
    place = lax.axis_index("local")
    core = lax.rem(node, 2)
    y = lax.rem(node // 2, 8)
    z_hi = node // 16
    z_lo = place // 4
    x_at = lax.rem(place, 4)
    high = [lax.rem(z_hi + step, 4) for step in BLOCK_STEPS]
    low = [z_lo, 1 - z_lo]

    def y_peer(d):
        return (z_hi * 16 + lax.rem(y + d, 8) * 2 + core, place)

    def z_peer(k, m):
        return (high[k] * 16 + y * 2 + core, low[m] * 4 + x_at)

    def place_peer(k):
        return (node, lax.rem(place + k, 8))

    partner = (node + 1 - 2 * core, place)
    z_slots = [(k, m) for k in range(4) for m in range(2) if (k, m) != (3, 0)]
    barrier = pltpu.get_barrier_semaphore()
    peers = [partner] + [y_peer(d) for d in range(1, 8)] + [z_peer(k, m) for k, m in z_slots]
    peers += [place_peer(k) for k in range(1, 8)]
    for peer in peers:
        pl.semaphore_signal(barrier, inc=1, device_id=peer, device_id_type=MESH)

    loads = [pltpu.make_async_copy(x_hbm, x, x_sem), pltpu.make_async_copy(gain_hbm, gain, gain_sem)]
    block_loads = []
    for k in range(4):
        columns = pl.ds(pl.multiple_of(high[k] * WIDTH, WIDTH), WIDTH)
        block_loads.append([
            pltpu.make_async_copy(weight_hbm.at[:, columns], weight.at[k], weight_sem.at[k]),
            pltpu.make_async_copy(cotangent_hbm.at[:, columns], cotangent.at[k], cotangent_sem.at[k]),
        ])
    for copy in [loads[0], *block_loads[0], loads[1], *block_loads[1], *block_loads[2], *block_loads[3]]:
        copy.start()

    def send(source, target, sends, recvs, peer):
        copy = pltpu.make_async_remote_copy(
            src_ref=source, dst_ref=target, send_sem=sends, recv_sem=recvs, device_id=peer, device_id_type=MESH
        )
        copy.start()
        return copy

    pairs, rings_a, rings_b, lasts, ends = {}, {}, {}, {}, []

    def compute(k):
        for copy in block_loads[k]:
            copy.wait()
        columns = pl.ds(pl.multiple_of(high[k] * WIDTH, WIDTH), WIDTH)
        grad = conv_grad_of(x[...], weight[k], gain[columns].reshape(1, WIDTH), cotangent[k])
        product = lax.dot_general(grad, x[...], (((0,), (0,)), ((), ())), preferred_element_type=F32)
        term[k] = product.astype(BF16).reshape(8, 2, 2, 16, CIN)

    def pair_up(k):
        pairs[k] = send(term.at[k, :, 1 - core], pair.at[k], pair_send.at[k], pair_recv.at[k], partner)

    def first_sums(k):
        pairs[k].wait_recv()

        @pl.loop(0, 8)
        def _(i):
            total = (term[k, i, core].astype(F32) + pair[k, i].astype(F32)).astype(BF16)
            mine_a[k, i] = total[:, :, 0:256]
            mine_b[k, 0, i] = total[0, :, 256:512]
            mine_b[k, 1, i] = total[1, :, 256:512]

        for d in FAR_FIRST:
            rings_a[k, d] = send(
                mine_a.at[k, lax.rem(y + d, 8)], ring_a.at[k, d - 1],
                ring_a_send.at[k, d - 1], ring_a_recv.at[k, d - 1], y_peer(d),
            )
        for m in range(2):
            if (k, m) in z_slots:
                slot = z_slots.index((k, m))
                rings_b[slot] = send(
                    mine_b.at[k, low[m]], ring_b.at[slot], ring_b_send.at[slot], ring_b_recv.at[slot], z_peer(k, m)
                )

    for copy in loads:
        copy.wait()
    for k in range(4):
        compute(k)
        if k == 0:
            pl.semaphore_wait(barrier, len(peers))
        pair_up(k)
        if k > 0:
            first_sums(k - 1)
    first_sums(3)

    for k in range(4):
        for d in range(1, 8):
            rings_a[k, d].wait_recv()
        total = mine_a[k, y].astype(F32)
        for d in range(7):
            total += ring_a[k, d].astype(F32)
        part_a[k] = total.astype(BF16)
        for m in range(2):
            if (k, m) in z_slots:
                slot = z_slots.index((k, m))
                lasts["a", slot] = send(
                    part_a.at[k, low[m]], last_a.at[slot], last_send.at[0, slot], last_recv.at[0, slot], z_peer(k, m)
                )
    for slot in range(7):
        rings_b[slot].wait_recv()

    @pl.loop(0, 8)
    def _(i):
        total = mine_b[3, z_lo, i].astype(F32)
        for slot in range(7):
            total += ring_b[slot, i].astype(F32)
        part_b[i] = total.astype(BF16)

    for d in FAR_FIRST:
        lasts["b", d - 1] = send(
            part_b.at[lax.rem(y + d, 8)], last_b.at[d - 1], last_send.at[1, d - 1], last_recv.at[1, d - 1], y_peer(d)
        )
    for slot in range(7):
        lasts["a", slot].wait_recv()
    total = part_a[3, z_lo].astype(F32)
    for slot in range(7):
        total += last_a[slot].astype(F32)
    piece[:, 0:256] = total.astype(BF16)
    for slot in range(7):
        lasts["b", slot].wait_recv()
    total = part_b[y].astype(F32)
    for slot in range(7):
        total += last_b[slot].astype(F32)
    piece[:, 256:512] = total.astype(BF16)
    for k in range(1, 8):
        ends.append(send(piece, pieces.at[place], piece_send.at[k - 1], piece_recv.at[k - 1], place_peer(k)))
    pieces[place] = piece[...]
    for copy in ends:
        copy.wait_recv()
    for half in range(2):
        total = pieces[half * 4].astype(F32)
        for i in range(1, 4):
            total += pieces[half * 4 + i].astype(F32)
        out[half] = total
    for copy in [*pairs.values(), *rings_a.values(), *rings_b.values(), *lasts.values(), *ends]:
        copy.wait_send()


def summed_gradient(block_input, conv_weight, bn_gain, out_cotangent):
    dma = pltpu.SemaphoreType.DMA
    return pl.pallas_call(
        step_kernel,
        out_shape=jax.ShapeDtypeStruct((2, 16, 512), F32),
        in_specs=[pl.BlockSpec(memory_space=pl.ANY)] * 4,
        out_specs=pl.BlockSpec(memory_space=pltpu.VMEM),
        scratch_shapes=[
            pltpu.VMEM((ROWS, CIN), BF16),
            pltpu.VMEM((4, CIN, WIDTH), BF16),
            pltpu.VMEM((4 * WIDTH,), F32),
            pltpu.VMEM((4, ROWS, WIDTH), BF16),
            pltpu.VMEM((4, 8, 2, 2, 16, CIN), BF16),
            pltpu.VMEM((4, 8, 2, 16, CIN), BF16),
            pltpu.VMEM((4, 8, 2, 16, 256), BF16),
            pltpu.VMEM((4, 2, 8, 16, 256), BF16),
            pltpu.VMEM((4, 7, 2, 16, 256), BF16),
            pltpu.VMEM((7, 8, 16, 256), BF16),
            pltpu.VMEM((4, 2, 16, 256), BF16),
            pltpu.VMEM((8, 16, 256), BF16),
            pltpu.VMEM((7, 16, 256), BF16),
            pltpu.VMEM((7, 16, 256), BF16),
            pltpu.VMEM((16, 512), BF16),
            pltpu.VMEM((8, 16, 512), BF16),
            dma, dma((4,)), dma, dma((4,)),
            dma((4,)), dma((4,)), dma((4, 7)), dma((4, 7)), dma((7,)), dma((7,)),
            dma((2, 7)), dma((2, 7)), dma((7,)), dma((7,)),
        ],
        compiler_params=pltpu.CompilerParams(collective_id=0, has_side_effects=True),
    )(block_input, conv_weight, bn_gain, out_cotangent)


def local(block_input, conv_weight, bn_gain, out_cotangent, master_weight, velocity):
    gradient = summed_gradient(block_input, conv_weight, bn_gain, out_cotangent).reshape(32, 512)
    new_velocity = MOMENTUM * velocity + gradient + DECAY * master_weight
    new_weight = master_weight - RATE * new_velocity
    return (new_velocity, new_weight)


def solution(mesh):
    in_specs = (
        P(("node", "local"), None),
        P(),
        P(),
        P(("node", "local"), None),
        P("node", None),
        P("node", None),
    )
    out_specs = (P("node", None), P("node", None))
    return jax.shard_map(local, mesh=mesh, in_specs=in_specs, out_specs=out_specs, check_vma=False)
```

time: 744 us -> 43.3 us (0.06)
  waiting for transfers between devices: 697 us -> 0 us
  Pallas kernels: 0 us -> 41 us
  between operations: 13.8 us -> 0.67 us
  matrix products: 11.2 us -> 0 us
  other arithmetic: 11.3 us -> 1.51 us
    reduce_scatter x4 -> x0, waiting for transfers between devices: 602 us -> none  [reduce_shards(): return lax.psum_scatter(summed, 'node', scatter_dimension=1, tiled=True)]
    psum x1 -> x0, waiting for transfers between devices: 95.2 us -> none  [reduce_shards(): lax.psum(contribution.astype(jnp.bfloat16), 'local').astype(jnp.float32)]
    pallas_call x0 -> x1, Pallas kernels: none -> 41 us  [summed_gradient(): pl.pallas_call(step_kernel, out_shape=jax.ShapeDtypeStruct((2, 16, 512),...]
    dot_general x5 -> x0, matrix products: 11.2 us -> none  [the longest x4 9.14 us: local(): lax.dot_general(columns, block_input, contract, preferred_element_type=jn...]
    convert_element_type x5 -> x0, other arithmetic: 8.74 us -> none  [the longest x4 6.69 us: reduce_shards(): lax.psum(contribution.astype(jnp.bfloat16), 'local').astype(jnp.float32)]
  transfers between devices with their start and end apart: 5 -> 0, of which waited for: 5 -> 0; matrix products, arithmetic and copies ran while one was open for 1% -> 0% of each run, Pallas kernels for 0% -> 0%
where the time goes in v2:
time: 43.3 us; the launch traced here: 43.1 us
  Pallas kernels  41 us (95%)
  other arithmetic  1.51 us (3%)
  between operations  0.67 us (2%)
    pallas_call x1, Pallas kernels, summed_gradient(): pl.pallas_call(step_kernel, out_shape=jax.ShapeDtypeStruct((2, 16, 512),...  41 us
    sub x1, other arithmetic, local(): new_weight = master_weight - RATE * new_velocity  1.51 us

profile of v2, /device:TPU:1, one launch (start us, length us, event | category | flops | bytes accessed | tf_op | source)
XLA Modules:
  0.0 43.1 jit_solution(16514595086899727388)
XLA Ops:
  0.6 0.0 copy-start.1
  0.6 0.0 copy-start
  0.7 41.0 %shard_map.77 = f32[2,16,512]{2,1,0:T(8,128)} custom-call(bf16[392,512]{1,0:T(8,128)(2,1)} %x_hbm.1, bf16[512,2048]{1,0:T(8,128)(2,1)} %weight_hbm.1, f32[2048]{0:T(1024)} %gain_hbm.1, bf16[392,2048]{1,0:T(8,128)(2,1)} %cotangent_hbm.1), custom_call_target="tpu_custom_call" | custom-call | tf_op jit(solution)/shard_map/pallas_call | solution.py:186
  41.6 0.0 copy-done.1
  41.6 0.0 copy-done
  41.6 1.5 %multiply_subtract_fusion = (f32[32,512]{1,0:T(8,128)}, f32[32,512]{1,0:T(8,128)}) fusion(f32[32,512]{1,0:T(8,128)S(1)} %copy-done, f32[2,16,512]{2,1,0:T(8,128)} %shard_map.77, f32[32,512]{1,0:T(8,128)S(1)} %copy-done.1), kind=kLoop, calls=%fused_computation.2 | loop fusion | flops 98304 | bytes 327680 | tf_op jit(solution)/shard_map/sub | solution.py:219
Async XLA Ops:
  0.6 41.0 %copy-start.1 = (f32[32,512]{1,0:T(8,128)S(1)}, f32[32,512]{1,0:T(8,128)}, u32[]{:S(2)}) copy-start(f32[32,512]{1,0:T(8,128)} %param.11) | copy-start | bytes 196612
  0.6 41.0 %copy-start = (f32[32,512]{1,0:T(8,128)S(1)}, f32[32,512]{1,0:T(8,128)}, u32[]{:S(2)}) copy-start(f32[32,512]{1,0:T(8,128)} %param.10) | copy-start | bytes 196612

commit v3 on v2

--- a/solution.py
+++ b/solution.py
@@ -33,8 +33,8 @@
 
 def step_kernel(
     x_hbm, weight_hbm, gain_hbm, cotangent_hbm, out, x, weight, gain, cotangent,
-    term, pair, mine_a, mine_b, ring_a, ring_b, part_a, part_b, last_a, last_b, piece, pieces,
-    x_sem, weight_sem, gain_sem, cotangent_sem, pair_send, pair_recv, ring_a_send, ring_a_recv, ring_b_send, ring_b_recv,
+    term, pair, mine_a, mine_b, inbox_a, inbox_b, relay_a, relay_b, part_a, part_b, last_a, last_b, piece, pieces,
+    x_sem, weight_sem, gain_sem, cotangent_sem, pair_send, pair_recv, a_send, a_recv, b_send, b_recv,
     last_send, last_recv, piece_send, piece_recv,
 ):
     node = lax.axis_index("node")
@@ -46,6 +46,8 @@
     x_at = lax.rem(place, 4)
     high = [lax.rem(z_hi + step, 4) for step in BLOCK_STEPS]
     low = [z_lo, 1 - z_lo]
+    z = z_hi * 2 + z_lo
+    turn = 1 - 2 * core
 
     def y_peer(d):
         return (z_hi * 16 + lax.rem(y + d, 8) * 2 + core, place)
@@ -53,17 +55,18 @@
     def z_peer(k, m):
         return (high[k] * 16 + y * 2 + core, low[m] * 4 + x_at)
 
+    def z_step(d):
+        to_z = lax.rem(z + d + 8, 8)
+        return ((to_z // 2) * 16 + y * 2 + core, lax.rem(to_z, 2) * 4 + x_at)
+
+    def y_step(d):
+        return lax.rem(y + d * turn + 8, 8)
+
     def place_peer(k):
         return (node, lax.rem(place + k, 8))
 
     partner = (node + 1 - 2 * core, place)
     z_slots = [(k, m) for k in range(4) for m in range(2) if (k, m) != (3, 0)]
-    barrier = pltpu.get_barrier_semaphore()
-    peers = [partner] + [y_peer(d) for d in range(1, 8)] + [z_peer(k, m) for k, m in z_slots]
-    peers += [place_peer(k) for k in range(1, 8)]
-    for peer in peers:
-        pl.semaphore_signal(barrier, inc=1, device_id=peer, device_id_type=MESH)
-
     loads = [pltpu.make_async_copy(x_hbm, x, x_sem), pltpu.make_async_copy(gain_hbm, gain, gain_sem)]
     block_loads = []
     for k in range(4):
@@ -75,6 +78,12 @@
     for copy in [loads[0], *block_loads[0], loads[1], *block_loads[1], *block_loads[2], *block_loads[3]]:
         copy.start()
 
+    barrier = pltpu.get_barrier_semaphore()
+    peers = [partner] + [y_peer(d) for d in range(1, 8)] + [z_peer(k, m) for k, m in z_slots]
+    peers += [place_peer(k) for k in range(1, 8)]
+    for peer in peers:
+        pl.semaphore_signal(barrier, inc=1, device_id=peer, device_id_type=MESH)
+
     def send(source, target, sends, recvs, peer):
         copy = pltpu.make_async_remote_copy(
             src_ref=source, dst_ref=target, send_sem=sends, recv_sem=recvs, device_id=peer, device_id_type=MESH
@@ -105,17 +114,86 @@
             mine_b[k, 0, i] = total[0, :, 256:512]
             mine_b[k, 1, i] = total[1, :, 256:512]
 
-        for d in FAR_FIRST:
-            rings_a[k, d] = send(
-                mine_a.at[k, lax.rem(y + d, 8)], ring_a.at[k, d - 1],
-                ring_a_send.at[k, d - 1], ring_a_recv.at[k, d - 1], y_peer(d),
-            )
+        for slot, (hop, d) in enumerate(((2, 4), (1, 3), (-1, -3), (1, 1), (-1, -1))):
+            send_a(k, slot, mine_a.at[k, y_step(d)], hop)
+        if k == 0:
+            send_b(0, mine_b.at[0, z_lo], 0, 2)
+        if k < 3:
+            slot, hop = ((2 - z_lo, 2 * z_lo - 1), (1 + 2 * z_lo, 1), (4 - 2 * z_lo, -1))[k]
+        else:
+            slot, hop = 3 + z_lo, 1 - 2 * z_lo
+        send_b(1 + k, mine_b.at[k, 1 - z_lo], slot, hop)
+
+    def send_a(k, slot, source, hop):
+        rings_a[k, slot] = send(
+            source, inbox_a.at[k, slot], a_send.at[k, slot], a_recv.at[k, slot],
+            (z_hi * 16 + y_step(hop) * 2 + core, place),
+        )
+
+    def send_b(index, source, slot, hop):
+        rings_b[index] = send(source, inbox_b.at[slot], b_send.at[index], b_recv.at[slot], z_step(hop))
+
+    def got_a(k, slot):
+        rings_a[k, slot].wait_recv()
+        return inbox_a[k, slot].astype(F32)
+
+    def relay_sums_a(k):
+        relay_a[k, 0] = (mine_a[k, y_step(2)].astype(F32) + got_a(k, 0) + got_a(k, 1)).astype(BF16)
+        send_a(k, 5, relay_a.at[k, 0], 2)
+        relay_a[k, 1] = (mine_a[k, y_step(-2)].astype(F32) + got_a(k, 2)).astype(BF16)
+        send_a(k, 6, relay_a.at[k, 1], -2)
+
+    def wait_b(slot):
+        pltpu.make_async_remote_copy(
+            src_ref=inbox_b.at[slot], dst_ref=inbox_b.at[slot], send_sem=b_send.at[0], recv_sem=b_recv.at[slot],
+            device_id=z_step(1), device_id_type=MESH,
+        ).wait_recv()
+
+    def relay_sums_b():
+        wait_b(0)
+        wait_b(1)
+
+        @pl.loop(0, 8)
+        def _(i):
+            total = mine_b[1, z_lo, i].astype(F32) + inbox_b[0, i].astype(F32) + inbox_b[1, i].astype(F32)
+            relay_b[0, i] = total.astype(BF16)
+
+        send_b(5, relay_b.at[0], 5, 2)
+        wait_b(2)
+
+        @pl.loop(0, 8)
+        def _(i):
+            relay_b[1, i] = (mine_b[2, z_lo, i].astype(F32) + inbox_b[2, i].astype(F32)).astype(BF16)
+
+        send_b(6, relay_b.at[1], 6, -2)
+
+    def second_sums_a(k):
+        total = mine_a[k, y].astype(F32)
+        for slot in range(3, 7):
+            total += got_a(k, slot)
+        part_a[k] = total.astype(BF16)
         for m in range(2):
             if (k, m) in z_slots:
                 slot = z_slots.index((k, m))
-                rings_b[slot] = send(
-                    mine_b.at[k, low[m]], ring_b.at[slot], ring_b_send.at[slot], ring_b_recv.at[slot], z_peer(k, m)
+                lasts["a", slot] = send(
+                    part_a.at[k, low[m]], last_a.at[slot], last_send.at[0, slot], last_recv.at[0, slot], z_peer(k, m)
                 )
+
+    def second_sums_b():
+        for slot in range(3, 7):
+            wait_b(slot)
+
+        @pl.loop(0, 8)
+        def _(i):
+            total = mine_b[3, z_lo, i].astype(F32)
+            for slot in range(3, 7):
+                total += inbox_b[slot, i].astype(F32)
+            part_b[i] = total.astype(BF16)
+
+        for d in FAR_FIRST:
+            lasts["b", d - 1] = send(
+                part_b.at[lax.rem(y + d, 8)], last_b.at[d - 1], last_send.at[1, d - 1], last_recv.at[1, d - 1], y_peer(d)
+            )
 
     for copy in loads:
         copy.wait()
@@ -126,35 +204,17 @@
         pair_up(k)
         if k > 0:
             first_sums(k - 1)
+    relay_sums_a(0)
+    relay_sums_a(1)
     first_sums(3)
-
-    for k in range(4):
-        for d in range(1, 8):
-            rings_a[k, d].wait_recv()
-        total = mine_a[k, y].astype(F32)
-        for d in range(7):
-            total += ring_a[k, d].astype(F32)
-        part_a[k] = total.astype(BF16)
-        for m in range(2):
-            if (k, m) in z_slots:
-                slot = z_slots.index((k, m))
-                lasts["a", slot] = send(
-                    part_a.at[k, low[m]], last_a.at[slot], last_send.at[0, slot], last_recv.at[0, slot], z_peer(k, m)
-                )
-    for slot in range(7):
-        rings_b[slot].wait_recv()
-
-    @pl.loop(0, 8)
-    def _(i):
-        total = mine_b[3, z_lo, i].astype(F32)
-        for slot in range(7):
-            total += ring_b[slot, i].astype(F32)
-        part_b[i] = total.astype(BF16)
-
-    for d in FAR_FIRST:
-        lasts["b", d - 1] = send(
-            part_b.at[lax.rem(y + d, 8)], last_b.at[d - 1], last_send.at[1, d - 1], last_recv.at[1, d - 1], y_peer(d)
-        )
+    relay_sums_b()
+    relay_sums_a(2)
+    second_sums_a(0)
+    second_sums_a(1)
+    relay_sums_a(3)
+    second_sums_b()
+    second_sums_a(2)
+    second_sums_a(3)
     for slot in range(7):
         lasts["a", slot].wait_recv()
     total = part_a[3, z_lo].astype(F32)
@@ -185,7 +245,7 @@
     dma = pltpu.SemaphoreType.DMA
     return pl.pallas_call(
         step_kernel,
-        out_shape=jax.ShapeDtypeStruct((2, 16, 512), F32),
+        out_shape=pltpu.VMEM((2, 16, 512), F32),
         in_specs=[pl.BlockSpec(memory_space=pl.ANY)] * 4,
         out_specs=pl.BlockSpec(memory_space=pltpu.VMEM),
         scratch_shapes=[
@@ -199,6 +259,8 @@
             pltpu.VMEM((4, 2, 8, 16, 256), BF16),
             pltpu.VMEM((4, 7, 2, 16, 256), BF16),
             pltpu.VMEM((7, 8, 16, 256), BF16),
+            pltpu.VMEM((4, 2, 2, 16, 256), BF16),
+            pltpu.VMEM((2, 8, 16, 256), BF16),
             pltpu.VMEM((4, 2, 16, 256), BF16),
             pltpu.VMEM((8, 16, 256), BF16),
             pltpu.VMEM((7, 16, 256), BF16),

time: 43.3 us -> 39.3 us (0.908)
  Pallas kernels: 41 us -> 37.4 us
  other arithmetic: 1.51 us -> 0.67 us
    pallas_call x1, Pallas kernels: 41 us -> 37.4 us  [summed_gradient(): pl.pallas_call(step_kernel, out_shape=pltpu.VMEM((2, 16, 512), F32), in_s...]
    sub x1, other arithmetic: 1.51 us -> 0.67 us  [local(): new_weight = master_weight - RATE * new_velocity]
where the time goes in v3:
time: 39.3 us; the launch traced here: 38.8 us
  Pallas kernels  37.4 us (95%)
  other arithmetic  0.67 us (2%)
  between operations  0.67 us (2%)
    pallas_call x1, Pallas kernels, summed_gradient(): pl.pallas_call(step_kernel, out_shape=pltpu.VMEM((2, 16, 512), F32), in_s...  37.4 us

profile of v3, /device:TPU:1, one launch (start us, length us, event | category | flops | bytes accessed | tf_op | source)
XLA Modules:
  0.0 38.8 jit_solution(3997596631587579868)
XLA Ops:
  0.6 0.0 copy-start.1
  0.6 0.0 copy-start
  0.7 37.4 %shard_map.77 = f32[2,16,512]{2,1,0:T(8,128)S(1)} custom-call(bf16[392,512]{1,0:T(8,128)(2,1)} %x_hbm.1, bf16[512,2048]{1,0:T(8,128)(2,1)} %weight_hbm.1, f32[2048]{0:T(1024)} %gain_hbm.1, bf16[392,2048]{1,0:T(8,128)(2,1)} %cotangent_hbm.1), custom_call_target="tpu_custom_call" | custom-call | tf_op jit(solution)/shard_map/pallas_call | solution.py:246
  38.1 0.0 copy-done.1
  38.1 0.0 copy-done
  38.1 0.7 %multiply_subtract_fusion = (f32[32,512]{1,0:T(8,128)}, f32[32,512]{1,0:T(8,128)}) fusion(f32[32,512]{1,0:T(8,128)S(1)} %copy-done, f32[2,16,512]{2,1,0:T(8,128)S(1)} %shard_map.77, f32[32,512]{1,0:T(8,128)S(1)} %copy-done.1), kind=kLoop, calls=%fused_computation.2 | loop fusion | flops 98304 | bytes 327680 | tf_op jit(solution)/shard_map/sub | solution.py:281
Async XLA Ops:
  0.6 37.5 %copy-start.1 = (f32[32,512]{1,0:T(8,128)S(1)}, f32[32,512]{1,0:T(8,128)}, u32[]{:S(2)}) copy-start(f32[32,512]{1,0:T(8,128)} %param.11) | copy-start | bytes 196612
  0.6 37.5 %copy-start = (f32[32,512]{1,0:T(8,128)S(1)}, f32[32,512]{1,0:T(8,128)}, u32[]{:S(2)}) copy-start(f32[32,512]{1,0:T(8,128)} %param.10) | copy-start | bytes 196612

commit v4 on v3

--- a/solution.py
+++ b/solution.py
@@ -19,8 +19,7 @@
 WIDTH = 512
 
 
-def conv_grad_of(x, weight, gain, cotangent):
-    conv = jnp.dot(x, weight, preferred_element_type=F32)
+def conv_grad_of(conv, gain, cotangent):
     center = jnp.sum(conv, axis=0, keepdims=True) * (1.0 / ROWS)
     spread = conv - center
     inverse = lax.rsqrt(jnp.sum(spread * spread, axis=0, keepdims=True) * (1.0 / ROWS) + EPS)
@@ -48,6 +47,7 @@
     low = [z_lo, 1 - z_lo]
     z = z_hi * 2 + z_lo
     turn = 1 - 2 * core
+    apart = z_lo + core - 2 * z_lo * core
 
     def y_peer(d):
         return (z_hi * 16 + lax.rem(y + d, 8) * 2 + core, place)
@@ -79,8 +79,8 @@
         copy.start()
 
     barrier = pltpu.get_barrier_semaphore()
-    peers = [partner] + [y_peer(d) for d in range(1, 8)] + [z_peer(k, m) for k, m in z_slots]
-    peers += [place_peer(k) for k in range(1, 8)]
+    peers = [partner] + [y_peer(d) for d in range(1, 8)]
+    peers += [z_step(d) for d in (1, -1, 2, -2)] + [place_peer(k) for k in range(1, 8)]
     for peer in peers:
         pl.semaphore_signal(barrier, inc=1, device_id=peer, device_id_type=MESH)
 
@@ -93,11 +93,14 @@
 
     pairs, rings_a, rings_b, lasts, ends = {}, {}, {}, {}, []
 
-    def compute(k):
+    def conv_of(k):
         for copy in block_loads[k]:
             copy.wait()
+        return jnp.dot(x[...], weight[k], preferred_element_type=F32)
+
+    def finish(k, conv):
         columns = pl.ds(pl.multiple_of(high[k] * WIDTH, WIDTH), WIDTH)
-        grad = conv_grad_of(x[...], weight[k], gain[columns].reshape(1, WIDTH), cotangent[k])
+        grad = conv_grad_of(conv, gain[columns].reshape(1, WIDTH), cotangent[k])
         product = lax.dot_general(grad, x[...], (((0,), (0,)), ((), ())), preferred_element_type=F32)
         term[k] = product.astype(BF16).reshape(8, 2, 2, 16, CIN)
 
@@ -107,21 +110,23 @@
     def first_sums(k):
         pairs[k].wait_recv()
 
-        @pl.loop(0, 8)
-        def _(i):
+        for i in range(8):
             total = (term[k, i, core].astype(F32) + pair[k, i].astype(F32)).astype(BF16)
             mine_a[k, i] = total[:, :, 0:256]
             mine_b[k, 0, i] = total[0, :, 256:512]
             mine_b[k, 1, i] = total[1, :, 256:512]
 
-        for slot, (hop, d) in enumerate(((2, 4), (1, 3), (-1, -3), (1, 1), (-1, -1))):
-            send_a(k, slot, mine_a.at[k, y_step(d)], hop)
+        if k < 3:
+            for slot, (hop, d) in enumerate(((2, 4), (1, 3), (-1, -3), (1, 1), (-1, -1))):
+                send_a(k, slot, mine_a.at[k, y_step(d)], hop)
+        else:
+            for slot, d in enumerate((4, 3, -3, 2, -2, 1, -1)):
+                send_a(k, slot, mine_a.at[k, y_step(d)], d)
         if k == 0:
-            send_b(0, mine_b.at[0, z_lo], 0, 2)
-        if k < 3:
-            slot, hop = ((2 - z_lo, 2 * z_lo - 1), (1 + 2 * z_lo, 1), (4 - 2 * z_lo, -1))[k]
-        else:
-            slot, hop = 3 + z_lo, 1 - 2 * z_lo
+            send_b(0, mine_b.at[0, z_lo], 0, 2 * turn)
+        slot, hop = (
+            (2 - apart, 2 * z_lo - 1), (1 + 2 * z_lo + core, 1), (4 - 2 * z_lo - core, -1), (3 + apart, 1 - 2 * z_lo)
+        )[k]
         send_b(1 + k, mine_b.at[k, 1 - z_lo], slot, hop)
 
     def send_a(k, slot, source, hop):
@@ -153,23 +158,21 @@
         wait_b(0)
         wait_b(1)
 
-        @pl.loop(0, 8)
-        def _(i):
-            total = mine_b[1, z_lo, i].astype(F32) + inbox_b[0, i].astype(F32) + inbox_b[1, i].astype(F32)
+        for i in range(8):
+            total = mine_b[1 + core, z_lo, i].astype(F32) + inbox_b[0, i].astype(F32) + inbox_b[1, i].astype(F32)
             relay_b[0, i] = total.astype(BF16)
 
-        send_b(5, relay_b.at[0], 5, 2)
+        send_b(5, relay_b.at[0], 5, 2 * turn)
         wait_b(2)
 
-        @pl.loop(0, 8)
-        def _(i):
-            relay_b[1, i] = (mine_b[2, z_lo, i].astype(F32) + inbox_b[2, i].astype(F32)).astype(BF16)
-
-        send_b(6, relay_b.at[1], 6, -2)
+        for i in range(8):
+            relay_b[1, i] = (mine_b[2 - core, z_lo, i].astype(F32) + inbox_b[2, i].astype(F32)).astype(BF16)
+
+        send_b(6, relay_b.at[1], 6, -2 * turn)
 
     def second_sums_a(k):
         total = mine_a[k, y].astype(F32)
-        for slot in range(3, 7):
+        for slot in range(3 if k < 3 else 0, 7):
             total += got_a(k, slot)
         part_a[k] = total.astype(BF16)
         for m in range(2):
@@ -183,8 +186,7 @@
         for slot in range(3, 7):
             wait_b(slot)
 
-        @pl.loop(0, 8)
-        def _(i):
+        for i in range(8):
             total = mine_b[3, z_lo, i].astype(F32)
             for slot in range(3, 7):
                 total += inbox_b[slot, i].astype(F32)
@@ -195,23 +197,32 @@
                 part_b.at[lax.rem(y + d, 8)], last_b.at[d - 1], last_send.at[1, d - 1], last_recv.at[1, d - 1], y_peer(d)
             )
 
+    def send_pieces():
+        for k in range(1, 8):
+            ends.append(send(
+                piece, pieces.at[place],
+                piece_send.at[0, k - 1], piece_recv.at[0, k - 1], place_peer(k),
+            ))
+
     for copy in loads:
         copy.wait()
+    conv = conv_of(0)
     for k in range(4):
-        compute(k)
+        following = conv_of(k + 1) if k < 3 else None
+        finish(k, conv)
+        conv = following
         if k == 0:
             pl.semaphore_wait(barrier, len(peers))
         pair_up(k)
         if k > 0:
             first_sums(k - 1)
+    first_sums(3)
     relay_sums_a(0)
     relay_sums_a(1)
-    first_sums(3)
     relay_sums_b()
     relay_sums_a(2)
     second_sums_a(0)
     second_sums_a(1)
-    relay_sums_a(3)
     second_sums_b()
     second_sums_a(2)
     second_sums_a(3)
@@ -227,8 +238,7 @@
     for slot in range(7):
         total += last_b[slot].astype(F32)
     piece[:, 256:512] = total.astype(BF16)
-    for k in range(1, 8):
-        ends.append(send(piece, pieces.at[place], piece_send.at[k - 1], piece_recv.at[k - 1], place_peer(k)))
+    send_pieces()
     pieces[place] = piece[...]
     for copy in ends:
         copy.wait_recv()
@@ -269,7 +279,7 @@
             pltpu.VMEM((8, 16, 512), BF16),
             dma, dma((4,)), dma, dma((4,)),
             dma((4,)), dma((4,)), dma((4, 7)), dma((4, 7)), dma((7,)), dma((7,)),
-            dma((2, 7)), dma((2, 7)), dma((7,)), dma((7,)),
+            dma((2, 7)), dma((2, 7)), dma((2, 7)), dma((2, 7)),
         ],
         compiler_params=pltpu.CompilerParams(collective_id=0, has_side_effects=True),
     )(block_input, conv_weight, bn_gain, out_cotangent)

time: 39.3 us -> 38.1 us (0.969)
  the two profiles are of different devices: /device:TPU:1 before, /device:TPU:2 now
where the time goes in v4:
time: 38.1 us; the launch traced here: 38 us
  Pallas kernels  36.6 us (96%)
  other arithmetic  0.67 us (2%)
  between operations  0.67 us (2%)
    pallas_call x1, Pallas kernels, summed_gradient(): pl.pallas_call(step_kernel, out_shape=pltpu.VMEM((2, 16, 512), F32), in_s...  36.6 us

profile of v4, /device:TPU:2, one launch (start us, length us, event | category | flops | bytes accessed | tf_op | source)
XLA Modules:
  0.0 38.0 jit_solution(5063683853154337159)
XLA Ops:
  0.6 0.0 copy-start.1
  0.6 0.0 copy-start
  0.7 36.6 %shard_map.77 = f32[2,16,512]{2,1,0:T(8,128)S(1)} custom-call(bf16[392,512]{1,0:T(8,128)(2,1)} %x_hbm.1, bf16[512,2048]{1,0:T(8,128)(2,1)} %weight_hbm.1, f32[2048]{0:T(1024)} %gain_hbm.1, bf16[392,2048]{1,0:T(8,128)(2,1)} %cotangent_hbm.1), custom_call_target="tpu_custom_call" | custom-call | tf_op jit(solution)/shard_map/pallas_call | solution.py:256
  37.3 0.0 copy-done.1
  37.3 0.0 copy-done
  37.3 0.7 %multiply_subtract_fusion = (f32[32,512]{1,0:T(8,128)}, f32[32,512]{1,0:T(8,128)}) fusion(f32[32,512]{1,0:T(8,128)S(1)} %copy-done, f32[2,16,512]{2,1,0:T(8,128)S(1)} %shard_map.77, f32[32,512]{1,0:T(8,128)S(1)} %copy-done.1), kind=kLoop, calls=%fused_computation.2 | loop fusion | flops 98304 | bytes 327680 | tf_op jit(solution)/shard_map/sub | solution.py:291
Async XLA Ops:
  0.6 36.7 %copy-start.1 = (f32[32,512]{1,0:T(8,128)S(1)}, f32[32,512]{1,0:T(8,128)}, u32[]{:S(2)}) copy-start(f32[32,512]{1,0:T(8,128)} %param.11) | copy-start | bytes 196612
  0.6 36.7 %copy-start = (f32[32,512]{1,0:T(8,128)S(1)}, f32[32,512]{1,0:T(8,128)}, u32[]{:S(2)}) copy-start(f32[32,512]{1,0:T(8,128)} %param.10) | copy-start | bytes 196612

commit v5 on v4

--- a/solution.py
+++ b/solution.py
@@ -75,7 +75,7 @@
             pltpu.make_async_copy(weight_hbm.at[:, columns], weight.at[k], weight_sem.at[k]),
             pltpu.make_async_copy(cotangent_hbm.at[:, columns], cotangent.at[k], cotangent_sem.at[k]),
         ])
-    for copy in [loads[0], *block_loads[0], loads[1], *block_loads[1], *block_loads[2], *block_loads[3]]:
+    for copy in [loads[0], *block_loads[0], loads[1]]:
         copy.start()
 
     barrier = pltpu.get_barrier_semaphore()
@@ -83,6 +83,8 @@
     peers += [z_step(d) for d in (1, -1, 2, -2)] + [place_peer(k) for k in range(1, 8)]
     for peer in peers:
         pl.semaphore_signal(barrier, inc=1, device_id=peer, device_id_type=MESH)
+    for copy in [*block_loads[1], *block_loads[2], *block_loads[3]]:
+        copy.start()
 
     def send(source, target, sends, recvs, peer):
         copy = pltpu.make_async_remote_copy(
@@ -198,7 +200,7 @@
             )
 
     def send_pieces():
-        for k in range(1, 8):
+        for k in (2, 6, 1, 3, 5, 7, 4):
             ends.append(send(
                 piece, pieces.at[place],
                 piece_send.at[0, k - 1], piece_recv.at[0, k - 1], place_peer(k),
@@ -217,9 +219,9 @@
         if k > 0:
             first_sums(k - 1)
     first_sums(3)
+    relay_sums_b()
     relay_sums_a(0)
     relay_sums_a(1)
-    relay_sums_b()
     relay_sums_a(2)
     second_sums_a(0)
     second_sums_a(1)
@@ -240,6 +242,8 @@
     piece[:, 256:512] = total.astype(BF16)
     send_pieces()
     pieces[place] = piece[...]
+    for copy in [*pairs.values(), *rings_a.values(), *rings_b.values(), *lasts.values()]:
+        copy.wait_send()
     for copy in ends:
         copy.wait_recv()
     for half in range(2):
@@ -247,7 +251,7 @@
         for i in range(1, 4):
             total += pieces[half * 4 + i].astype(F32)
         out[half] = total
-    for copy in [*pairs.values(), *rings_a.values(), *rings_b.values(), *lasts.values(), *ends]:
+    for copy in ends:
         copy.wait_send()
 
 

time: 38.1 us -> 37.9 us (level)
  the two profiles are of different devices: /device:TPU:2 before, /device:TPU:8 now
where the time goes in v5:
time: 37.9 us; the launch traced here: 37.7 us
  Pallas kernels  36.4 us (96%)
  other arithmetic  0.67 us (2%)
  between operations  0.67 us (2%)
    pallas_call x1, Pallas kernels, summed_gradient(): pl.pallas_call(step_kernel, out_shape=pltpu.VMEM((2, 16, 512), F32), in_s...  36.4 us

profile of v5, /device:TPU:8, one launch (start us, length us, event | category | flops | bytes accessed | tf_op | source)
XLA Modules:
  0.0 37.7 jit_solution(1312151344473466035)
XLA Ops:
  0.6 0.0 copy-start.1
  0.6 0.0 copy-start
  0.7 36.4 %shard_map.77 = f32[2,16,512]{2,1,0:T(8,128)S(1)} custom-call(bf16[392,512]{1,0:T(8,128)(2,1)} %x_hbm.1, bf16[512,2048]{1,0:T(8,128)(2,1)} %weight_hbm.1, f32[2048]{0:T(1024)} %gain_hbm.1, bf16[392,2048]{1,0:T(8,128)(2,1)} %cotangent_hbm.1), custom_call_target="tpu_custom_call" | custom-call | tf_op jit(solution)/shard_map/pallas_call | solution.py:260
  37.0 0.0 copy-done.1
  37.0 0.0 copy-done
  37.0 0.7 %multiply_subtract_fusion = (f32[32,512]{1,0:T(8,128)}, f32[32,512]{1,0:T(8,128)}) fusion(f32[32,512]{1,0:T(8,128)S(1)} %copy-done, f32[2,16,512]{2,1,0:T(8,128)S(1)} %shard_map.77, f32[32,512]{1,0:T(8,128)S(1)} %copy-done.1), kind=kLoop, calls=%fused_computation.2 | loop fusion | flops 98304 | bytes 327680 | tf_op jit(solution)/shard_map/sub | solution.py:295
Async XLA Ops:
  0.6 36.4 %copy-start.1 = (f32[32,512]{1,0:T(8,128)S(1)}, f32[32,512]{1,0:T(8,128)}, u32[]{:S(2)}) copy-start(f32[32,512]{1,0:T(8,128)} %param.11) | copy-start | bytes 196612
  0.6 36.4 %copy-start = (f32[32,512]{1,0:T(8,128)S(1)}, f32[32,512]{1,0:T(8,128)}, u32[]{:S(2)}) copy-start(f32[32,512]{1,0:T(8,128)} %param.10) | copy-start | bytes 196612
